TPU v7x, 32 devices: a whole 2x2x4 slice. The times are simulated.
32 devices in a mesh: groups: 2 (over y), gz: 4 (over z), view: 2 (over x), gy: 2 (over core).
Axes of the slice: x: 2, y: 2, z: 4, core: 2. Of those that a mesh axis runs over, the one named last changes fastest.
Arguments:
- camera: float32 [2, 256, 3, 128, 128], P('view', ('groups', 'gz'), None, 'gy'), parts along dimension 1, may hold values from 0 to 4
- background: int32 [2, 2, 8], P('view', 'gy', ('groups', 'gz')), parts along dimension 2, may hold values from 0 to 2
- destination: int32 [2, 2, 256, 1], P('view', 'gy', ('groups', 'gz')), parts along dimension 2, may hold values from 0 to 3; in each aligned block of 32 rows (0 to 31, 32 to 63, ..., all dimensions but the last counted through in order) at most 16 rows name the same one
- offsets: int32 [2, 2, 256], P('view', 'gy', ('groups', 'gz')), parts along dimension 2, may hold values from 0 to 6
- shift_frac: float32 [2, 3], P('view'), may hold values from 0.15 to 0.85
- psf_taps: float32 [2, 3, 9], P('view'), may hold values from 0.05 to 1
Outputs:
- estimate: float32 [64, 128, 128], P(('groups', 'gz'), 'gy'), parts along dimension 0
- joined_views: float32 [2, 64, 128, 128], P('view', ('groups', 'gz'), 'gy'), parts along dimension 1
There are 2 independent parts, one for each index of `groups`. A program takes and returns all parts, laid end to end along the dimension named above; an argument that names none is the same for every part. Nothing has to cross between parts.
Inputs may be any that keep to these rules, and one draw needn't show every extreme that they name: `destination`: within the 32 block rows of one tile, no slab is named more than 16 times; some tile names one slab exactly 16 times.
All inputs are finite; a program needn't handle non-finite values.
Results may differ from a plain program's by a relative error of at most 0.0001.
Values sent between devices are 32-bit elements; how exact they have to be, the bound alone decides.
A program may use at most 64 MiB of HBM per device.

v0:
```python
import jax
import jax.numpy as jnp
from jax import lax
from jax.sharding import PartitionSpec as P

CZ = 8
ITERS = 2


DATA_FLOOR = 0.25
PRECISE = lax.Precision.HIGHEST


def extended(block, sides, width):
    for axis, dim in sides:
        count = lax.axis_size(axis)
        forward = [(i, i + 1) for i in range(count - 1)]
        backward = [(target, source) for source, target in forward]
        low = lax.ppermute(
            lax.slice_in_dim(block, block.shape[dim] - width, None, axis=dim), axis, forward
        )
        high = lax.ppermute(lax.slice_in_dim(block, 0, width, axis=dim), axis, backward)
        block = jnp.concatenate([low, block, high], axis=dim)
    return block


def interp_matrix(length, fraction):
    places = jnp.arange(length, dtype=jnp.int32)
    follow = jnp.minimum(places + 1, length - 1)
    same_row = (places[:, None] == places[None, :]).astype(jnp.float32)
    next_row = (follow[:, None] == places[None, :]).astype(jnp.float32)
    return (1.0 - fraction) * same_row + fraction * next_row


def interp_blocks(blocks, fraction_z, y_matrix, x_matrix):
    lower = blocks[..., :-1, :, :]
    upper = blocks[..., 1:, :, :]
    planes = (1.0 - fraction_z) * lower + fraction_z * upper
    planes = jnp.einsum("ry,...yx->...rx", y_matrix, planes, precision=PRECISE)
    return jnp.einsum("...rx,cx->...rc", planes, x_matrix, precision=PRECISE)


def along_last(volume, weights):
    margin = weights.shape[0] // 2
    span_cells = volume.shape[-1]
    padded = jnp.pad(volume, [(0, 0)] * (volume.ndim - 1) + [(margin, margin)])
    result = weights[0] * padded[..., 0:span_cells]
    for offset in range(1, weights.shape[0]):
        result = result + weights[offset] * padded[..., offset : offset + span_cells]
    return result


def valid_pass(padded, weights, out_len, along_axis):
    result = weights[0] * lax.slice_in_dim(padded, 0, out_len, axis=along_axis)
    for offset in range(1, weights.shape[0]):
        result = result + weights[offset] * lax.slice_in_dim(
            padded, offset, offset + out_len, axis=along_axis
        )
    return result


def apply_passes(padded, kernel, planes_out, rows_out):
    x_done = along_last(padded, kernel[2])
    y_done = valid_pass(x_done, kernel[1], rows_out, 1)
    return valid_pass(y_done, kernel[0], planes_out, 0)


def spread(volume, kernel):
    margin = kernel.shape[1] // 2
    padded = extended(volume, (("gz", 0), ("gy", 1)), margin)
    return apply_passes(padded, kernel, volume.shape[0], volume.shape[1])


def on_device(camera, background, destination, offsets, shift_frac, psf_taps):
    level = background[0, 0, 0].astype(jnp.float32)
    blocks = camera[0] - level
    block_count = blocks.shape[0]
    tile_rows = blocks.shape[2]
    tile_cols = blocks.shape[3]
    slabs = lax.axis_size("gz")
    most = max(2, 2 * block_count // slabs)
    target = destination[0, 0, :, 0]
    first_plane = offsets[0, 0]
    same_slab = target[:, None] == target[None, :]
    positions = jnp.arange(block_count, dtype=jnp.int32)
    earlier = positions[None, :] < positions[:, None]
    rank = jnp.sum((same_slab & earlier).astype(jnp.int32), axis=1)
    slot = target * most + rank
    select = (jnp.arange(slabs * most, dtype=jnp.int32)[:, None] == slot[None, :]).astype(
        jnp.float32
    )
    codes_out = jnp.dot(select, (first_plane + 1).astype(jnp.float32), precision=PRECISE).reshape(
        slabs, most
    )
    fraction = shift_frac[0]
    y_matrix = interp_matrix(tile_rows, fraction[1])
    x_matrix = interp_matrix(tile_cols, fraction[2])
    smoothed = interp_blocks(blocks, fraction[0], y_matrix, x_matrix)
    packed = jnp.dot(select, smoothed.reshape(block_count, -1), precision=PRECISE)
    packed = packed.reshape((slabs, most) + smoothed.shape[1:])
    planes, codes = (
        lax.all_to_all(packed, "gz", split_axis=0, concat_axis=0, tiled=True),
        lax.all_to_all(codes_out, "gz", split_axis=0, concat_axis=0, tiled=True),
    )
    plane_count = planes.shape[2]
    valid = (codes > 0.5)[:, :, None]
    landing = (codes - 1.0)[:, :, None] + jnp.arange(plane_count, dtype=jnp.float32)[None, None, :]
    valid_wide = jnp.broadcast_to(valid, landing.shape).reshape(1, -1)
    deposit = (jnp.arange(CZ, dtype=jnp.float32)[:, None] == landing.reshape(1, -1)) & valid_wide
    deposit = deposit.astype(jnp.float32)
    total = jnp.dot(deposit, planes.reshape(-1, tile_rows * tile_cols), precision=PRECISE).reshape(
        CZ, tile_rows, tile_cols
    )
    covered = jnp.sum(deposit, axis=1)
    joined = jnp.maximum(total / (covered[:, None, None] + 1.0), DATA_FLOOR)
    kernel = psf_taps[0] / jnp.sum(psf_taps[0], axis=-1, keepdims=True)
    flipped = kernel[:, ::-1]
    view_count = lax.axis_size("view")
    estimate = lax.psum(joined, "view") / view_count
    for iteration in range(ITERS):
        blurred = spread(estimate, kernel)
        ratio = joined / blurred
        correction = spread(ratio, flipped)
        logs = jnp.log(correction)
        log_total = lax.psum(logs, "view")
        estimate = estimate * jnp.exp(log_total / view_count)
    return (estimate, joined[None])


def solution(mesh):
    return jax.shard_map(
        on_device,
        mesh=mesh,
        in_specs=(
            P("view", ("groups", "gz"), None, "gy", None),
            P("view", "gy", ("groups", "gz")),
            P("view", "gy", ("groups", "gz"), None),
            P("view", "gy", ("groups", "gz")),
            P("view", None),
            P("view", None, None),
        ),
        out_specs=(P(("groups", "gz"), "gy", None), P("view", ("groups", "gz"), "gy", None)),
        check_vma=False,
    )
```

profile of v0, /device:TPU:8, one launch (start us, length us, event | category | flops | bytes accessed | tf_op | source)
XLA Modules:
  0.0 364.1 jit_solution(4947907883737901542)
XLA Ops:
  8.7 1.5 convolution_bitcast_fusion
  10.3 5.3 %all-to-all-start = ((f32[4,1,16]{2,1,0:T(1,128)}), f32[4,1,16]{2,1,0:T(1,128)S(1)}, u32[]{:S(2)}, u32[]{:S(2)}) async-start(f32[4,1,16]{2,1,0:T(1,128)} %convolution_bitcast_fusion), calls=%async_computation | async-start | bytes 4096 | tf_op jit(solution)/shard_map/all_to_all | solution.py:103
  15.6 1.4 fusion.181
  19.6 2.2 subtract_bitcast_fusion
  21.8 3.6 fusion.1
  25.4 2.6 fusion.5
  29.6 5.2 %fusion.3 = f32[4,16,2,64,128]{4,1,3,2,0:T(8,128)} fusion(f32[2,64,128,32]{2,1,0,3:T(8,128)S(1)} %bitcast.103, s32[32]{0:T(128)S(1)} %multiply_add_fusion.1, s32[4,16]{1,0:T(4,128)S(1)} %multiply_add_fusion), kind=kOutput, calls=%fused_computation.39 | convolution fusion | flops 402655232 | bytes 6291840 | tf_op jit(solution)/shard_map/dot_general | solution.py:99
  34.8 5.1 %all-to-all-start.1 = ((f32[4,16,2,64,128]{4,1,3,2,0:T(8,128)}), f32[4,16,2,64,128]{4,1,3,2,0:T(8,128)}, u32[]{:S(2)}, u32[]{:S(2)}) async-start(f32[4,16,2,64,128]{4,1,3,2,0:T(8,128)} %fusion.3), calls=%async_computation.1 | async-start | bytes 8388608 | tf_op jit(solution)/shard_map/all_to_all | solution.py:102
  40.5 89.0 %all-to-all-done.1 = f32[4,16,2,64,128]{4,1,3,2,0:T(8,128)} async-done(((f32[4,16,2,64,128]{4,1,3,2,0:T(8,128)}), f32[4,16,2,64,128]{4,1,3,2,0:T(8,128)}, u32[]{:S(2)}, u32[]{:S(2)}) %all-to-all-start.1) | async-done | bytes 4194336 | tf_op jit(solution)/shard_map/all_to_all | solution.py:102
  129.5 3.5 copy.29
  133.0 5.2 %copy.50 = f32[16,8,64,128]{3,1,2,0:T(8,128)} copy(f32[16,8,64,128]{3,2,1,0:T(8,128)S(1)} %bitcast.101) | data formatting | bytes 8388608
  138.2 5.7 %copy.30 = f32[8192,128]{1,0:T(8,128)} copy(f32[8192,128]{0,1:T(8,128)} %bitcast.102) | data formatting | bytes 8388608 | tf_op jit(solution)/shard_map/dot_general | solution.py:111
  143.9 4.9 %fusion.8 = f32[8,64,128]{2,0,1:T(8,128)} fusion(f32[64,128,128]{2,1,0:T(8,128)} %bitcast.100, f32[8]{0:T(128)S(1)} %broadcast_add_fusion.1, f32[128]{0:T(128)S(1)} %add.390, pred[128]{0:T(512)(128)(4,1)S(1)} %and.14), kind=kOutput, calls=%fused_computation.45 | convolution fusion | flops 100796416 | bytes 4457120 | tf_op jit(solution)/shard_map/dot_general | solution.py:111
  149.0 25.2 %all-reduce.8.cloned.1.call-done = f32[8,64,128]{2,0,1:T(8,128)} async-done(((f32[8,64,128]{2,0,1:T(8,128)}), f32[8,64,128]{2,0,1:T(8,128)}) %all-reduce.8.cloned.1.call-update) | async-done | bytes 262160 | tf_op jit(solution)/shard_map/psum | solution.py:119
  175.2 3.4 collective-permute-start
  178.6 2.5 collective-permute-start.1
  182.1 3.4 collective-permute-done.1
  186.8 1.3 collective-permute-start.3
  190.0 6.9 %fusion.19 = f32[16,72,128]{2,0,1:T(8,128)S(1)} fusion(f32[16,72,128]{2,0,1:T(8,128)S(1)} %pad_maximum_fusion, f32[]{:T(128)} %bitcast.37, f32[]{:T(128)} %bitcast.36, f32[]{:T(128)} %bitcast.35, f32[]{:T(128)} %bitcast.34, f32[]{:T(128)} %bitcast.33, f32[]{:T(128)} %bitcast.32, f32[]{:T(128)} %bitcast.31, f32[]{:T(128)} %bitcast.30, f32[]{:T(128)} %bitcast.27), kind=kLoop, calls=%fused_computation.57 | loop fusion | flops 2506752 | bytes 1179684 | tf_op jit(solution)/shard_map/add | solution.py:49
  196.9 6.0 %fusion.99 = f32[16,64,128]{2,0,1:T(8,128)S(1)} fusion(f32[16,72,128]{2,0,1:T(8,128)S(1)} %fusion.19, f32[]{:T(128)} %bitcast.44, f32[]{:T(128)} %bitcast.43, f32[]{:T(128)} %bitcast.42, f32[]{:T(128)} %bitcast.41, f32[]{:T(128)} %bitcast.40, f32[]{:T(128)} %bitcast.39, f32[]{:T(128)} %bitcast.38, f32[]{:T(128)} %bitcast.29, f32[]{:T(128)} %bitcast.26), kind=kLoop, calls=%fused_computation.169 | loop fusion | flops 2228224 | bytes 5242916 | tf_op jit(solution)/shard_map/add | solution.py:56
  203.0 5.8 %fusion.135 = f32[8,64,128]{2,0,1:T(8,128)S(1)} fusion(f32[8,64,128]{2,0,1:T(8,128)S(1)} %copy-done, f32[16,64,128]{2,0,1:T(8,128)S(1)} %fusion.99, f32[]{:T(128)} %bitcast.51, f32[]{:T(128)} %bitcast.50, f32[]{:T(128)} %bitcast.49, f32[]{:T(128)} %bitcast.48, f32[]{:T(128)} %bitcast.47, f32[]{:T(128)} %bitcast.46, f32[]{:T(128)} %bitcast.45, f32[]{:T(128)} %bitcast.28, ...), kind=kLoop, calls=%fused_computation.241 | loop fusion | flops 1179648 | bytes 2883620 | tf_op jit(solution)/shard_map/div | solution.py:122
  208.8 3.4 collective-permute-start.4
  212.2 2.5 collective-permute-start.5
  214.7 1.6 collective-permute-done.4
  216.3 3.1 collective-permute-done.5
  220.7 1.5 collective-permute-start.7
  222.3 1.6 collective-permute-done.7
  223.9 6.9 %fusion.35 = f32[16,72,128]{2,0,1:T(8,128)S(1)} fusion(f32[16,72,128]{2,0,1:T(8,128)S(1)} %pad_maximum_fusion.1, f32[]{:T(128)} %bitcast.37, f32[]{:T(128)} %bitcast.36, f32[]{:T(128)} %bitcast.35, f32[]{:T(128)} %bitcast.34, f32[]{:T(128)} %bitcast.33, f32[]{:T(128)} %bitcast.32, f32[]{:T(128)} %bitcast.31, f32[]{:T(128)} %bitcast.30, f32[]{:T(128)} %bitcast.27), kind=kLoop, calls=%fused_computation.73 | loop fusion | flops 2506752 | bytes 1179684 | tf_op jit(solution)/shard_map/add | solution.py:49
  230.9 6.0 %fusion.91 = f32[16,64,128]{2,0,1:T(8,128)S(1)} fusion(f32[16,72,128]{2,0,1:T(8,128)S(1)} %fusion.35, f32[]{:T(128)} %bitcast.44, f32[]{:T(128)} %bitcast.43, f32[]{:T(128)} %bitcast.42, f32[]{:T(128)} %bitcast.41, f32[]{:T(128)} %bitcast.40, f32[]{:T(128)} %bitcast.39, f32[]{:T(128)} %bitcast.38, f32[]{:T(128)} %bitcast.29, f32[]{:T(128)} %bitcast.26), kind=kLoop, calls=%fused_computation.152 | loop fusion | flops 2228224 | bytes 5242916 | tf_op jit(solution)/shard_map/add | solution.py:56
  236.9 6.6 %fusion.126 = f32[8,64,128]{2,0,1:T(8,128)} fusion(f32[16,64,128]{2,0,1:T(8,128)S(1)} %fusion.91, f32[]{:T(128)} %bitcast.51, f32[]{:T(128)} %bitcast.50, f32[]{:T(128)} %bitcast.49, f32[]{:T(128)} %bitcast.48, f32[]{:T(128)} %bitcast.47, f32[]{:T(128)} %bitcast.46, f32[]{:T(128)} %bitcast.45, f32[]{:T(128)} %bitcast.28, f32[]{:T(128)} %bitcast.25), kind=kLoop, calls=%fused_computation.223 | loop fusion | flops 1114112 | bytes 2621476 | tf_op jit(solution)/shard_map/log | solution.py:124
  243.5 21.6 %all-reduce.10.cloned.1.call-done = f32[8,64,128]{2,0,1:T(8,128)} async-done(((f32[8,64,128]{2,0,1:T(8,128)}), f32[8,64,128]{2,0,1:T(8,128)}) %all-reduce.10.cloned.1.call-update) | async-done | bytes 262160 | tf_op jit(solution)/shard_map/psum | solution.py:125
  266.1 3.4 collective-permute-start.8
  269.5 2.5 collective-permute-start.9
  273.0 3.4 collective-permute-done.9
  277.7 1.3 collective-permute-start.11
  279.0 1.8 collective-permute-done.11
  280.9 6.9 %fusion.51 = f32[16,72,128]{2,0,1:T(8,128)S(1)} fusion(f32[16,72,128]{2,0,1:T(8,128)S(1)} %pad_maximum_fusion.2, f32[]{:T(128)} %bitcast.37, f32[]{:T(128)} %bitcast.36, f32[]{:T(128)} %bitcast.35, f32[]{:T(128)} %bitcast.34, f32[]{:T(128)} %bitcast.33, f32[]{:T(128)} %bitcast.32, f32[]{:T(128)} %bitcast.31, f32[]{:T(128)} %bitcast.30, f32[]{:T(128)} %bitcast.27), kind=kLoop, calls=%fused_computation.89 | loop fusion | flops 2506752 | bytes 1179684 | tf_op jit(solution)/shard_map/add | solution.py:49
  287.9 6.0 %fusion.83 = f32[16,64,128]{2,0,1:T(8,128)S(1)} fusion(f32[16,72,128]{2,0,1:T(8,128)S(1)} %fusion.51, f32[]{:T(128)} %bitcast.44, f32[]{:T(128)} %bitcast.43, f32[]{:T(128)} %bitcast.42, f32[]{:T(128)} %bitcast.41, f32[]{:T(128)} %bitcast.40, f32[]{:T(128)} %bitcast.39, f32[]{:T(128)} %bitcast.38, f32[]{:T(128)} %bitcast.29, f32[]{:T(128)} %bitcast.26), kind=kLoop, calls=%fused_computation.135 | loop fusion | flops 2228224 | bytes 5242916 | tf_op jit(solution)/shard_map/add | solution.py:56
  293.8 5.8 %fusion.117 = f32[8,64,128]{2,0,1:T(8,128)S(1)} fusion(f32[8,64,128]{2,0,1:T(8,128)S(1)} %copy-done, f32[16,64,128]{2,0,1:T(8,128)S(1)} %fusion.83, f32[]{:T(128)} %bitcast.51, f32[]{:T(128)} %bitcast.50, f32[]{:T(128)} %bitcast.49, f32[]{:T(128)} %bitcast.48, f32[]{:T(128)} %bitcast.47, f32[]{:T(128)} %bitcast.46, f32[]{:T(128)} %bitcast.45, f32[]{:T(128)} %bitcast.28, ...), kind=kLoop, calls=%fused_computation.205 | loop fusion | flops 1179648 | bytes 2883620 | tf_op jit(solution)/shard_map/div | solution.py:122
  299.7 3.4 collective-permute-start.12
  303.1 2.5 collective-permute-start.13
  305.6 1.6 collective-permute-done.12
  307.1 3.1 collective-permute-done.13
  312.9 1.8 collective-permute-done.15
  314.8 6.9 %fusion.67 = f32[16,72,128]{2,0,1:T(8,128)S(1)} fusion(f32[16,72,128]{2,0,1:T(8,128)S(1)} %pad_maximum_fusion.3, f32[]{:T(128)} %bitcast.37, f32[]{:T(128)} %bitcast.36, f32[]{:T(128)} %bitcast.35, f32[]{:T(128)} %bitcast.34, f32[]{:T(128)} %bitcast.33, f32[]{:T(128)} %bitcast.32, f32[]{:T(128)} %bitcast.31, f32[]{:T(128)} %bitcast.30, f32[]{:T(128)} %bitcast.27), kind=kLoop, calls=%fused_computation.105 | loop fusion | flops 2506752 | bytes 1179684 | tf_op jit(solution)/shard_map/add | solution.py:49
  321.7 6.0 %fusion.75 = f32[16,64,128]{2,0,1:T(8,128)S(1)} fusion(f32[16,72,128]{2,0,1:T(8,128)S(1)} %fusion.67, f32[]{:T(128)} %bitcast.44, f32[]{:T(128)} %bitcast.43, f32[]{:T(128)} %bitcast.42, f32[]{:T(128)} %bitcast.41, f32[]{:T(128)} %bitcast.40, f32[]{:T(128)} %bitcast.39, f32[]{:T(128)} %bitcast.38, f32[]{:T(128)} %bitcast.29, f32[]{:T(128)} %bitcast.26), kind=kLoop, calls=%fused_computation.118 | loop fusion | flops 2228224 | bytes 5242916 | tf_op jit(solution)/shard_map/add | solution.py:56
  327.7 6.5 %fusion.108 = f32[8,64,128]{2,0,1:T(8,128)} fusion(f32[16,64,128]{2,0,1:T(8,128)S(1)} %fusion.75, f32[]{:T(128)} %bitcast.51, f32[]{:T(128)} %bitcast.50, f32[]{:T(128)} %bitcast.49, f32[]{:T(128)} %bitcast.48, f32[]{:T(128)} %bitcast.47, f32[]{:T(128)} %bitcast.46, f32[]{:T(128)} %bitcast.45, f32[]{:T(128)} %bitcast.28, f32[]{:T(128)} %bitcast.25), kind=kLoop, calls=%fused_computation.187 | loop fusion | flops 1114112 | bytes 2621476 | tf_op jit(solution)/shard_map/log | solution.py:124
  335.0 20.9 %all-reduce.12.cloned.1.call-done = f32[8,64,128]{2,0,1:T(8,128)} async-done(((f32[8,64,128]{2,0,1:T(8,128)}), f32[8,64,128]{2,0,1:T(8,128)}) %all-reduce.12.cloned.1.call-update) | async-done | bytes 262160 | tf_op jit(solution)/shard_map/psum | solution.py:125
  (62 shorter events, 19.4 us)
Async XLA Ops:
  10.3 24.5 %all-to-all-start = ((f32[4,1,16]{2,1,0:T(1,128)}), f32[4,1,16]{2,1,0:T(1,128)S(1)}, u32[]{:S(2)}, u32[]{:S(2)}) async-start(f32[4,1,16]{2,1,0:T(1,128)} %convolution_bitcast_fusion), calls=%async_computation | async-start | bytes 4096 | tf_op jit(solution)/shard_map/all_to_all | solution.py:103
  34.8 94.7 %all-to-all-start.1 = ((f32[4,16,2,64,128]{4,1,3,2,0:T(8,128)}), f32[4,16,2,64,128]{4,1,3,2,0:T(8,128)}, u32[]{:S(2)}, u32[]{:S(2)}) async-start(f32[4,16,2,64,128]{4,1,3,2,0:T(8,128)} %fusion.3), calls=%async_computation.1 | async-start | bytes 8388608 | tf_op jit(solution)/shard_map/all_to_all | solution.py:102
  39.9 134.3 %all-reduce.8.cloned.1.call-start = ((), (), s32[]{:S(2)}) async-start(), calls=%async_computation.2 | async-start | bytes 524288 | tf_op jit(solution)/shard_map/psum | solution.py:119
  143.9 5.0 %copy-start.2 = (f32[1,3,9]{2,0,1:T(1,128)S(1)}, f32[1,3,9]{2,0,1:T(1,128)}, u32[]{:S(2)}) copy-start(f32[1,3,9]{2,0,1:T(1,128)} %param.11) | copy-start | bytes 328
  148.8 116.3 %all-reduce.10.cloned.1.call-start = ((), (), s32[]{:S(2)}) async-start(), calls=%async_computation.3 | async-start | bytes 524288 | tf_op jit(solution)/shard_map/psum | solution.py:125
  175.2 6.9 %collective-permute-start = (f32[4,64,128]{2,0,1:T(4,128)S(1)}, f32[4,64,128]{2,0,1:T(4,128)S(1)}, u32[]{:S(2)}, u32[]{:S(2)}) collective-permute-start(f32[4,64,128]{2,0,1:T(4,128)S(1)} %get-tuple-element.26), channel_id=1, source_target_pairs={{0,4},{4,8},{8,12},{1,5},{5,9},{9,13},{2,6},{6,10},{10,14},{3,7},{... | collective-permute-start | bytes 393224 | tf_op jit(solution)/shard_map/ppermute | solution.py:19
  178.6 6.9 %collective-permute-start.1 = (f32[4,64,128]{2,0,1:T(4,128)S(1)}, f32[4,64,128]{2,0,1:T(4,128)S(1)}, u32[]{:S(2)}, u32[]{:S(2)}) collective-permute-start(f32[4,64,128]{2,0,1:T(4,128)S(1)} %get-tuple-element.27), channel_id=1, source_target_pairs={{4,0},{8,4},{12,8},{5,1},{9,5},{13,9},{6,2},{10,6},{14,10},{7,3},{... | collective-permute-start | bytes 393224 | tf_op jit(solution)/shard_map/ppermute | solution.py:22
  185.5 3.3 collective-permute-start.2
  186.8 3.1 collective-permute-start.3
  196.9 6.0 %copy-start = (f32[8,64,128]{2,0,1:T(8,128)S(1)}, f32[8,64,128]{2,0,1:T(8,128)}, u32[]{:S(2)}) copy-start(f32[8,64,128]{2,0,1:T(8,128)} %fusion.8) | copy-start | bytes 786436
  208.8 7.5 %collective-permute-start.4 = (f32[4,64,128]{2,0,1:T(4,128)S(1)}, f32[4,64,128]{2,0,1:T(4,128)S(1)}, u32[]{:S(2)}, u32[]{:S(2)}) collective-permute-start(f32[4,64,128]{2,0,1:T(4,128)S(1)} %get-tuple-element.24), channel_id=1, source_target_pairs={{0,4},{4,8},{8,12},{1,5},{5,9},{9,13},{2,6},{6,10},{10,14},{3,7},{... | collective-permute-start | bytes 393224 | tf_op jit(solution)/shard_map/ppermute | solution.py:19
  212.2 7.2 %collective-permute-start.5 = (f32[4,64,128]{2,0,1:T(4,128)S(1)}, f32[4,64,128]{2,0,1:T(4,128)S(1)}, u32[]{:S(2)}, u32[]{:S(2)}) collective-permute-start(f32[4,64,128]{2,0,1:T(4,128)S(1)} %get-tuple-element.25), channel_id=1, source_target_pairs={{4,0},{8,4},{12,8},{5,1},{9,5},{13,9},{6,2},{10,6},{14,10},{7,3},{... | collective-permute-start | bytes 393224 | tf_op jit(solution)/shard_map/ppermute | solution.py:22
  219.4 2.8 collective-permute-start.6
  220.7 3.1 collective-permute-start.7
  236.8 28.2 %copy-start.1 = (f32[8,64,128]{2,0,1:T(8,128)S(1)}, f32[8,64,128]{2,0,1:T(8,128)}, u32[]{:S(2)}) copy-start(f32[8,64,128]{2,0,1:T(8,128)} %all-reduce.8.cloned.1.call-done) | copy-start | bytes 786436
  243.5 112.4 %all-reduce.12.cloned.1.call-start = ((), (), s32[]{:S(2)}) async-start(), calls=%async_computation.4 | async-start | bytes 524288 | tf_op jit(solution)/shard_map/psum | solution.py:125
  266.1 6.9 %collective-permute-start.8 = (f32[4,64,128]{2,0,1:T(4,128)S(1)}, f32[4,64,128]{2,0,1:T(4,128)S(1)}, u32[]{:S(2)}, u32[]{:S(2)}) collective-permute-start(f32[4,64,128]{2,0,1:T(4,128)S(1)} %get-tuple-element.22), channel_id=1, source_target_pairs={{0,4},{4,8},{8,12},{1,5},{5,9},{9,13},{2,6},{6,10},{10,14},{3,7},{... | collective-permute-start | bytes 393224 | tf_op jit(solution)/shard_map/ppermute | solution.py:19
  269.5 6.9 %collective-permute-start.9 = (f32[4,64,128]{2,0,1:T(4,128)S(1)}, f32[4,64,128]{2,0,1:T(4,128)S(1)}, u32[]{:S(2)}, u32[]{:S(2)}) collective-permute-start(f32[4,64,128]{2,0,1:T(4,128)S(1)} %get-tuple-element.23), channel_id=1, source_target_pairs={{4,0},{8,4},{12,8},{5,1},{9,5},{13,9},{6,2},{10,6},{14,10},{7,3},{... | collective-permute-start | bytes 393224 | tf_op jit(solution)/shard_map/ppermute | solution.py:22
  276.4 2.6 collective-permute-start.10
  277.7 3.1 collective-permute-start.11
  299.7 7.5 %collective-permute-start.12 = (f32[4,64,128]{2,0,1:T(4,128)S(1)}, f32[4,64,128]{2,0,1:T(4,128)S(1)}, u32[]{:S(2)}, u32[]{:S(2)}) collective-permute-start(f32[4,64,128]{2,0,1:T(4,128)S(1)} %get-tuple-element.20), channel_id=1, source_target_pairs={{0,4},{4,8},{8,12},{1,5},{5,9},{9,13},{2,6},{6,10},{10,14},{3,7},{... | collective-permute-start | bytes 393224 | tf_op jit(solution)/shard_map/ppermute | solution.py:19
  303.1 7.2 %collective-permute-start.13 = (f32[4,64,128]{2,0,1:T(4,128)S(1)}, f32[4,64,128]{2,0,1:T(4,128)S(1)}, u32[]{:S(2)}, u32[]{:S(2)}) collective-permute-start(f32[4,64,128]{2,0,1:T(4,128)S(1)} %get-tuple-element.21), channel_id=1, source_target_pairs={{4,0},{8,4},{12,8},{5,1},{9,5},{13,9},{6,2},{10,6},{14,10},{7,3},{... | collective-permute-start | bytes 393224 | tf_op jit(solution)/shard_map/ppermute | solution.py:22
  310.3 2.6 collective-permute-start.14
  311.6 3.1 collective-permute-start.15
Sparse Core Ops, SparseCore 0:
  148.9 25.2 all-reduce.7
  243.6 21.4 all-reduce.9
  334.4 21.4 all-reduce.11
where the time goes:
time: 368 us; the launch traced here: 364 us
  waiting for transfers between devices  180 us (49%)
  other arithmetic  83.9 us (23%)
  starting transfers between devices  44.4 us (12%)
  local copies, waits for them, and re-layouts  20.8 us (6%)
  matrix products  17.8 us (5%)
  between operations  16.7 us (5%)
    all_to_all x1, waiting for transfers between devices, on_device(): lax.all_to_all(packed, 'gz', split_axis=0, concat_axis=0, tiled=True)  89 us
    psum x2, waiting for transfers between devices, on_device(): log_total = lax.psum(logs, 'view')  42.4 us
    add x4, other arithmetic, along_last(): result = result + weights[offset] * padded[..., offset:offset + span_cells]  27.7 us
    psum x1, waiting for transfers between devices, on_device(): estimate = lax.psum(joined, 'view') / view_count  25.2 us
    add x4, other arithmetic, valid_pass(): result + weights[offset] * lax.slice_in_dim(padded, offset, offset + out_...  23.9 us
    ppermute x8, waiting for transfers between devices, extended(): lax.ppermute(lax.slice_in_dim(block, 0, width, axis=dim), axis, backward)  19.3 us
    ppermute x8, starting transfers between devices, extended(): lax.ppermute(lax.slice_in_dim(block, block.shape[dim] - width, None, axis...  18.7 us
    ppermute x8, starting transfers between devices, extended(): lax.ppermute(lax.slice_in_dim(block, 0, width, axis=dim), axis, backward)  15.2 us
  transfers between devices with their start and end apart: 21, of which 16 were waited for; matrix products, arithmetic and copies ran while one was open for 5% of the time, Pallas kernels for 0%

commit v1 on v0

v1 whole, which is shorter than its diff:
```python
import functools

import jax
import jax.numpy as jnp
from jax import lax
from jax.experimental import pallas as pl
from jax.experimental.pallas import tpu as pltpu
from jax.sharding import PartitionSpec as P

CZ = 8
ITERS = 2
HALO = 8
CHUNK = 4

DATA_FLOOR = 0.25
PRECISE = lax.Precision.HIGHEST
MESH = pl.DeviceIdType.MESH


def deposit_kernel(rows, dest, offs, level, frac, psf, cam_ref, acc_ref, tap_ref):
    step = pl.program_id(0)
    taps = psf.shape[1]

    @pl.when(step == 0)
    def _():
        @pl.loop(0, acc_ref.shape[0])
        def _(s):
            acc_ref[s] = jnp.zeros(acc_ref.shape[1:], jnp.float32)

        tap_ref[...] = jnp.zeros(tap_ref.shape, jnp.float32)
        for axis in range(3):
            scale = psf[axis, 0]
            for t in range(1, taps):
                scale = scale + psf[axis, t]
            scale = jnp.full((1, 128), scale, jnp.float32)
            for t in range(taps):
                at = axis * taps + t
                tap_ref[at : at + 1, :] = jnp.full((1, 128), psf[axis, t], jnp.float32) / scale

    fz = frac[0]
    base = level[0].astype(jnp.float32)
    for i in range(cam_ref.shape[0]):
        b = step * cam_ref.shape[0] + i
        s = dest[b]
        o = offs[b]
        lower = cam_ref[i, 0] - base
        for k in range(cam_ref.shape[1] - 1):
            upper = cam_ref[i, k + 1] - base
            at = pl.ds(pl.multiple_of((o + k) * rows, 8), rows)
            acc_ref[s, at, :] = acc_ref[s, at, :] + ((1.0 - fz) * lower + fz * upper)
            cnt = pl.ds(CZ * rows + o + k, 1)
            acc_ref[s, cnt, :] = acc_ref[s, cnt, :] + 1.0
            lower = upper


def world_kernel(
    dims, rows, taps,
    frac, acc_ref, tap_in, est_ref, joined_ref,
    recv, tap_all, jx, e0, e1, kx, za, zb, rt, yb, lg,
    a2a_s, a2a_r, own_sem, tap_s, tap_r, row_s, row_r, lo_s, lo_r, hi_s, hi_r, loc_sem,
    zs, zr, es, er, out_s, out_r,
):
    slabs, views, bands = dims
    strip = rows // views
    wide = strip + 2 * HALO
    margin = taps // 2
    z = lax.axis_index("gz")
    v = lax.axis_index("view")
    g = lax.axis_index("gy")

    def snake(band, place):
        return jnp.where(band % 2 == 1, views - 1 - place, place)

    idx = snake(g, v)
    me = g * views + idx
    strips = views * bands

    def dev(zz, vv, gg):
        return {"gz": zz, "view": vv, "gy": gg}

    def strip_dev(zz, ss):
        band = ss // views
        return dev(zz, snake(band, ss % views), band)

    below, above = z > 0, z < slabs - 1
    left, right = me > 0, me < strips - 1

    @pl.loop(0, views)
    def _(w):
        @pl.loop(0, 3 * CZ)
        def _(p):
            jx[w, p] = jnp.zeros((wide, 128), jnp.float32)

    @pl.loop(0, 3 * CZ)
    def _(p):
        e1[p] = jnp.zeros((wide, 128), jnp.float32)

    barrier = pltpu.get_barrier_semaphore()

    def greet(target):
        pl.semaphore_signal(barrier, inc=1, device_id=target, device_id_type=MESH)

    for d in range(1, slabs):
        greet(dev((z + d) % slabs, v, g))
    for d in range(1, strips):
        greet(strip_dev(z, (me + d) % strips))
    corners = []
    for dz, zok in ((-1, below), (1, above)):
        for ds, sok in ((-1, left), (1, right)):
            corners.append((dz, ds, zok & sok))
    amount = slabs - 1 + strips - 1
    for dz, ds, ok in corners:
        amount = amount + ok.astype(jnp.int32)

        @pl.when(ok)
        def _(dz=dz, ds=ds):
            greet(strip_dev(z + dz, me + ds))

    pl.semaphore_wait(barrier, amount)

    def a2a(d):
        to = (z + d) % slabs
        return pltpu.make_async_remote_copy(
            src_ref=acc_ref.at[to], dst_ref=recv.at[d - 1], send_sem=a2a_s.at[d - 1],
            recv_sem=a2a_r.at[d - 1], device_id=dev(to, v, g), device_id_type=MESH)

    for d in range(1, slabs):
        a2a(d).start()
    own = pltpu.make_async_copy(acc_ref.at[z], recv.at[slabs - 1], own_sem)
    own.start()
    own_tap = pltpu.make_async_copy(tap_in, tap_all.at[v], loc_sem.at[1])
    own_tap.start()

    def tap_copy(d):
        return pltpu.make_async_remote_copy(
            src_ref=tap_in, dst_ref=tap_all.at[v], send_sem=tap_s.at[d - 1],
            recv_sem=tap_r.at[d - 1], device_id={"view": (v + d) % views}, device_id_type=MESH)

    for d in range(1, views):
        tap_copy(d).start()
    own_tap.wait()
    for d in range(1, views):
        tap_copy(d).wait()

    apart = lax.broadcasted_iota(jnp.int32, (128, 128), 0) - lax.broadcasted_iota(jnp.int32, (128, 128), 1)

    @pl.loop(0, views)
    def _(w):
        ahead = jnp.zeros((128, 128), jnp.float32)
        back = jnp.zeros((128, 128), jnp.float32)
        for t in range(taps):
            tap = tap_all[w, 2 * taps + t : 2 * taps + t + 1, :]
            ahead = jnp.where(apart == t - margin, tap, ahead)
            back = jnp.where(apart == margin - t, tap, back)
        kx[w, 0] = ahead
        kx[w, 1] = back

    own.wait()
    for d in range(1, slabs):
        a2a(d).wait_recv()

    fy, fx = frac[1], frac[2]
    last_row = lax.broadcasted_iota(jnp.int32, (rows, 128), 0) == rows - 1
    last_col = lax.broadcasted_iota(jnp.int32, (rows, 128), 1) == 127

    @pl.loop(0, CZ)
    def _(p):
        at = pl.ds(pl.multiple_of(p * rows, 8), rows)
        cnt = pl.ds(CZ * rows + p, 1)
        total = recv[0, at, :]
        covered = recv[0, cnt, :]
        for s in range(1, slabs):
            total = total + recv[s, at, :]
            covered = covered + recv[s, cnt, :]
        follow = jnp.where(last_row, total, pltpu.roll(total, rows - 1, 0))
        total = (1.0 - fy) * total + fy * follow
        follow = jnp.where(last_col, total, pltpu.roll(total, 127, 1))
        total = (1.0 - fx) * total + fx * follow
        joined_ref[0, p] = jnp.maximum(total / (covered + 1.0), DATA_FLOOR)

    joined = joined_ref.at[0]
    mid = pl.ds(CZ, CZ)

    def main_piece(i):
        lo, hi = max(i * strip - HALO, 0), min((i + 1) * strip + HALO, rows)
        return pl.ds(lo, hi - lo), pl.ds(lo - i * strip + HALO, hi - lo)

    def main_copy(i, target, sem_at):
        src, dst = main_piece(i)
        return pltpu.make_async_remote_copy(
            src_ref=joined.at[:, src, :], dst_ref=jx.at[v, mid, dst, :], send_sem=row_s.at[i],
            recv_sem=row_r.at[sem_at], device_id={"view": target}, device_id_type=MESH)

    def main_local(i):
        src, dst = main_piece(i)
        return pltpu.make_async_copy(joined.at[:, src, :], jx.at[v, mid, dst, :], loc_sem.at[0])

    def edge_copy(up):
        src = pl.ds(rows - HALO, HALO) if up else pl.ds(0, HALO)
        dst = pl.ds(0, HALO) if up else pl.ds(HALO + strip, HALO)
        sems = (lo_s, lo_r) if up else (hi_s, hi_r)
        target = strip_dev(z, (g + 1) * views if up else g * views - 1)
        return pltpu.make_async_remote_copy(
            src_ref=joined.at[:, src, :], dst_ref=jx.at[v, mid, dst, :], send_sem=sems[0],
            recv_sem=sems[1].at[v], device_id=target, device_id_type=MESH)

    for i in range(views):
        owner = snake(g, i)

        @pl.when(owner != v)
        def _(i=i, owner=owner):
            main_copy(i, owner, v).start()

        @pl.when(owner == v)
        def _(i=i):
            main_local(i).start()

    next_band, prev_band = g < bands - 1, g > 0

    @pl.when(next_band)
    def _():
        edge_copy(True).start()

    @pl.when(prev_band)
    def _():
        edge_copy(False).start()

    def z_copy(w, up):
        dst = pl.ds(0, CZ) if up else pl.ds(2 * CZ, CZ)
        side = 1 if up else 0
        return pltpu.make_async_remote_copy(
            src_ref=jx.at[w, mid], dst_ref=jx.at[w, dst], send_sem=zs.at[side, w],
            recv_sem=zr.at[side, w], device_id={"gz": z + 1 if up else z - 1}, device_id_type=MESH)

    for d in range(views):
        w = (v + d) % views
        for i in range(views):
            if d == 0:
                @pl.when(idx == i)
                def _(i=i):
                    main_local(i).wait()
            else:
                @pl.when(idx == i)
                def _(i=i, w=w):
                    main_copy(i, v, w).wait_recv()

        @pl.when((idx == 0) & prev_band)
        def _(w=w):
            pltpu.make_async_remote_copy(
                src_ref=joined.at[:, pl.ds(rows - HALO, HALO), :], dst_ref=jx.at[w, mid, pl.ds(0, HALO), :],
                send_sem=lo_s, recv_sem=lo_r.at[w], device_id={"view": v}, device_id_type=MESH).wait_recv()

        @pl.when((idx == views - 1) & next_band)
        def _(w=w):
            pltpu.make_async_remote_copy(
                src_ref=joined.at[:, pl.ds(0, HALO), :], dst_ref=jx.at[w, mid, pl.ds(HALO + strip, HALO), :],
                send_sem=hi_s, recv_sem=hi_r.at[w], device_id={"view": v}, device_id_type=MESH).wait_recv()

        @pl.when(above)
        def _(w=w):
            z_copy(w, True).start()

        @pl.when(below)
        def _(w=w):
            z_copy(w, False).start()

    for d in range(views):
        w = (v + d) % views

        @pl.when(below)
        def _(w=w):
            z_copy(w, True).wait_recv()

        @pl.when(above)
        def _(w=w):
            z_copy(w, False).wait_recv()

    @pl.loop(0, 3 * CZ)
    def _(p):
        total = jx[0, p]
        for w in range(1, views):
            total = total + jx[w, p]
        e0[p] = total / views

    planes_r = CZ + 2 * margin
    rows_r = strip + 2 * margin

    def correct(est):
        for w in range(views):
            def tap(axis, t):
                at = axis * taps + t
                return tap_all[w, at : at + 1, :]

            @pl.loop(0, planes_r)
            def _(p):
                total = tap(0, 0) * est[p + CZ - 2 * margin]
                for t in range(1, taps):
                    total = total + tap(0, t) * est[p + CZ - 2 * margin + t]
                za[p] = total
                base = HALO - 2 * margin
                total = tap(1, 0) * za[p, base : base + rows_r, :]
                for t in range(1, taps):
                    total = total + tap(1, t) * za[p, base + t : base + t + rows_r, :]
                zb[p] = total

            @pl.loop(0, planes_r // 4)
            def _(c):
                at = pl.ds(c * 4, 4)
                blurred = jnp.dot(
                    zb[at].reshape(4 * rows_r, 128), kx[w, 0], precision=PRECISE,
                    preferred_element_type=jnp.float32).reshape(4, rows_r, 128)
                data = jx[w, pl.ds(c * 4 + CZ - margin, 4), HALO - margin : HALO - margin + rows_r, :]
                rt[at] = jnp.where(data > 0.0, data / blurred, 0.0)

            @pl.loop(0, CZ)
            def _(p):
                total = tap(0, taps - 1) * rt[p]
                for t in range(1, taps):
                    total = total + tap(0, taps - 1 - t) * rt[p + t]
                za[p, 0:rows_r, :] = total
                total = tap(1, taps - 1) * za[p, 0:strip, :]
                for t in range(1, taps):
                    total = total + tap(1, taps - 1 - t) * za[p, t : t + strip, :]
                yb[p] = total

            @pl.loop(0, CZ // 4)
            def _(c):
                at = pl.ds(c * 4, 4)
                logs = jnp.log(jnp.dot(
                    yb[at].reshape(4 * strip, 128), kx[w, 1], precision=PRECISE,
                    preferred_element_type=jnp.float32)).reshape(4, strip, 128)
                lg[at] = logs if w == 0 else lg[at] + logs

    inner = pl.ds(HALO, strip)
    near = []
    for n, (dz, ds) in enumerate([(a, b) for a in (-1, 0, 1) for b in (-1, 0, 1) if a or b]):
        zok = {-1: below, 0: z >= 0, 1: above}[dz]
        sok = {-1: left, 0: z >= 0, 1: right}[ds]
        far_z = {-1: above, 0: z >= 0, 1: below}[dz]
        far_s = {-1: right, 0: z >= 0, 1: left}[ds]
        near.append((n, dz, ds, zok & sok, far_z & far_s))

    def near_copy(n, dz, ds):
        src_r = {-1: pl.ds(HALO, HALO), 0: inner, 1: pl.ds(strip, HALO)}[ds]
        dst_r = {-1: pl.ds(HALO + strip, HALO), 0: inner, 1: pl.ds(0, HALO)}[ds]
        dst_p = {-1: pl.ds(2 * CZ, CZ), 0: mid, 1: pl.ds(0, CZ)}[dz]
        return pltpu.make_async_remote_copy(
            src_ref=e1.at[mid, src_r, :], dst_ref=e1.at[dst_p, dst_r, :], send_sem=es.at[n],
            recv_sem=er.at[n], device_id=strip_dev(z + dz, me + ds), device_id_type=MESH)

    def out_copy(target, sem_at):
        at = pl.ds(pl.multiple_of(idx * strip, 8), strip)
        return pltpu.make_async_remote_copy(
            src_ref=lg, dst_ref=est_ref.at[:, at, :], send_sem=out_s.at[sem_at],
            recv_sem=out_r.at[sem_at], device_id={"view": target}, device_id_type=MESH)

    correct(e0)
    for p in range(CZ):
        e1[CZ + p, inner, :] = e0[CZ + p, inner, :] * jnp.exp(lg[p] / views)
    for n, dz, ds, ok, _ in near:
        @pl.when(ok)
        def _(n=n, dz=dz, ds=ds):
            near_copy(n, dz, ds).start()
    for n, dz, ds, _, ok in near:
        @pl.when(ok)
        def _(n=n, dz=dz, ds=ds):
            near_copy(n, dz, ds).wait_recv()

    correct(e1)
    mine = pl.ds(pl.multiple_of(idx * strip, 8), strip)
    for p in range(CZ):
        done = e1[CZ + p, inner, :] * jnp.exp(lg[p] / views)
        lg[p] = done
        est_ref[p, mine, :] = done
    for d in range(1, views):
        out_copy((v + d) % views, d - 1).start()
    for d in range(1, views):
        out_copy((v + d) % views, d - 1).wait()

    for d in range(1, slabs):
        a2a(d).wait_send()
    for i in range(views):
        owner = snake(g, i)

        @pl.when(owner != v)
        def _(i=i, owner=owner):
            main_copy(i, owner, v).wait_send()

    @pl.when(next_band)
    def _():
        edge_copy(True).wait_send()

    @pl.when(prev_band)
    def _():
        edge_copy(False).wait_send()

    for w in range(views):
        @pl.when(above)
        def _(w=w):
            z_copy(w, True).wait_send()

        @pl.when(below)
        def _(w=w):
            z_copy(w, False).wait_send()

    for n, dz, ds, ok, _ in near:
        @pl.when(ok)
        def _(n=n, dz=dz, ds=ds):
            near_copy(n, dz, ds).wait_send()


def on_device(dims, camera, background, destination, offsets, shift_frac, psf_taps):
    slabs, views, bands = dims
    blocks, planes, rows, cols = camera.shape[1:]
    taps = psf_taps.shape[-1]
    margin = taps // 2
    tall = CZ * rows + CZ
    strip = rows // views
    wide = strip + 2 * HALO
    tap_rows = -(-3 * taps // 8) * 8
    smem = pl.BlockSpec(memory_space=pltpu.SMEM)
    acc, tap_rows_all = pl.pallas_call(
        functools.partial(deposit_kernel, rows),
        grid=(blocks // CHUNK,),
        in_specs=[smem] * 5 + [pl.BlockSpec((CHUNK, planes, rows, cols), lambda i: (i, 0, 0, 0))],
        out_specs=(
            pl.BlockSpec((slabs, tall, cols), lambda i: (0, 0, 0)),
            pl.BlockSpec((tap_rows, cols), lambda i: (0, 0)),
        ),
        out_shape=(
            jax.ShapeDtypeStruct((slabs, tall, cols), jnp.float32),
            jax.ShapeDtypeStruct((tap_rows, cols), jnp.float32),
        ),
        name="deposit",
    )(destination.reshape(-1), offsets.reshape(-1), background.reshape(-1), shift_frac[0], psf_taps[0], camera[0])

    vmem = pl.BlockSpec(memory_space=pltpu.VMEM)
    dma = pltpu.SemaphoreType.DMA
    f32 = jnp.float32
    estimate, joined = pl.pallas_call(
        functools.partial(world_kernel, dims, rows, taps),
        in_specs=[smem, pl.BlockSpec(memory_space=pl.ANY), vmem],
        out_specs=(vmem, vmem),
        out_shape=(
            jax.ShapeDtypeStruct((CZ, rows, cols), f32),
            jax.ShapeDtypeStruct((1, CZ, rows, cols), f32),
        ),
        scratch_shapes=[
            pltpu.VMEM((slabs, tall, cols), f32),
            pltpu.VMEM((views, tap_rows, cols), f32),
            pltpu.VMEM((views, 3 * CZ, wide, cols), f32),
            pltpu.VMEM((3 * CZ, wide, cols), f32),
            pltpu.VMEM((3 * CZ, wide, cols), f32),
            pltpu.VMEM((views, 2, cols, cols), f32),
            pltpu.VMEM((CZ + 2 * margin, wide, cols), f32),
            pltpu.VMEM((CZ + 2 * margin, strip + 2 * margin, cols), f32),
            pltpu.VMEM((CZ + 2 * margin, strip + 2 * margin, cols), f32),
            pltpu.VMEM((CZ, strip, cols), f32),
            pltpu.VMEM((CZ, strip, cols), f32),
            dma((slabs,)), dma((slabs,)), dma, dma((views,)), dma((views,)),
            dma((views,)), dma((views,)), dma, dma((views,)), dma, dma((views,)), dma((2,)),
            dma((2, views)), dma((2, views)), dma((8,)), dma((8,)), dma((views,)), dma((views,)),
        ],
        compiler_params=pltpu.CompilerParams(
            collective_id=0, has_side_effects=True, vmem_limit_bytes=40 * 1024 * 1024),
        name="world",
    )(shift_frac[0], acc, tap_rows_all)
    return estimate, joined


def solution(mesh):
    dims = (mesh.shape["gz"], mesh.shape["view"], mesh.shape["gy"])
    return jax.shard_map(
        functools.partial(on_device, dims),
        mesh=mesh,
        in_specs=(
            P("view", ("groups", "gz"), None, "gy", None),
            P("view", "gy", ("groups", "gz")),
            P("view", "gy", ("groups", "gz"), None),
            P("view", "gy", ("groups", "gz")),
            P("view", None),
            P("view", None, None),
        ),
        out_specs=(P(("groups", "gz"), "gy", None), P("view", ("groups", "gz"), "gy", None)),
        check_vma=False,
    )
```

time: 368 us -> 72.7 us (0.20)
  waiting for transfers between devices: 180 us -> 0 us
  other arithmetic: 83.9 us -> 0 us
  Pallas kernels: 0 us -> 66.5 us
  starting transfers between devices: 44.4 us -> 0 us
  matrix products: 17.8 us -> 0 us
  local copies, waits for them, and re-layouts: 20.8 us -> 4.62 us
  between operations: 16.7 us -> 1.31 us
    all_to_all x2 -> x0, waiting for transfers between devices: 89 us -> none  [the longest x1 89 us: on_device(): lax.all_to_all(packed, 'gz', split_axis=0, concat_axis=0, tiled=True)]
    psum x3 -> x0, waiting for transfers between devices: 67.7 us -> none  [the longest x2 42.4 us: on_device(): log_total = lax.psum(logs, 'view')]
    pallas_call x0 -> x2, Pallas kernels: none -> 66.5 us  [the longest x1 60.8 us: on_device(): pl.pallas_call(functools.partial(world_kernel, dims, rows, taps), in_spec...]
    add x11 -> x0, other arithmetic: 52.4 us -> none  [the longest x4 27.7 us: along_last(): result = result + weights[offset] * padded[..., offset:offset + span_cells]]
    ppermute x16 -> x0, starting transfers between devices: 33.9 us -> none  [the longest x8 18.7 us: extended(): lax.ppermute(lax.slice_in_dim(block, block.shape[dim] - width, None, axis...]
    ppermute x16 -> x0, waiting for transfers between devices: 23.7 us -> none  [the longest x8 19.3 us: extended(): lax.ppermute(lax.slice_in_dim(block, 0, width, axis=dim), axis, backward)]
    dot_general x5 -> x0, matrix products: 17.8 us -> none  [the longest x1 5.21 us: on_device(): jnp.dot(select, smoothed.reshape(block_count, -1), precision=PRECISE)]
    log x2 -> x0, other arithmetic: 13.1 us -> none  [on_device(): logs = jnp.log(correction)]
  transfers between devices with their start and end apart: 21 -> 0, of which waited for: 16 -> 0; matrix products, arithmetic and copies ran while one was open for 5% -> 0% of each run, Pallas kernels for 0% -> 0%
where the time goes in v1:
time: 72.7 us; the launch traced here: 72.4 us
  Pallas kernels  66.5 us (91%)
  local copies, waits for them, and re-layouts  4.62 us (6%)
  between operations  1.31 us (2%)
    pallas_call x1, Pallas kernels, on_device(): pl.pallas_call(functools.partial(world_kernel, dims, rows, taps), in_spec...  60.8 us
    pallas_call x1, Pallas kernels, on_device(): pl.pallas_call(functools.partial(deposit_kernel, rows), grid=(blocks // C...  5.69 us
    unnamed x9, local copies, waits for them, and re-layouts  4.62 us

profile of v1, /device:TPU:8, one launch (start us, length us, event | category | flops | bytes accessed | tf_op | source)
XLA Modules:
  0.0 72.4 jit_solution(13509454087999709815)
XLA Ops:
  0.6 0.0 copy-start.2
  1.3 1.3 %copy.10 = f32[1,3,9]{2,1,0:T(4,128)} copy(f32[1,3,9]{2,0,1:T(1,128)} %param.11) | data formatting | bytes 216
  2.6 5.7 %deposit.1 = (f32[4,520,128]{2,1,0:T(8,128)}, f32[32,128]{1,0:T(8,128)}) custom-call(s32[32]{0:T(128)} %bitcast.13, s32[32]{0:T(128)} %bitcast.14, s32[1]{0:T(128)} %bitcast.8.level, f32[3]{0:T(128)} %bitcast.9, f32[3,9]{1,0:T(4,128)} %bitcast.12, f32[32,3,64,128]{3,2,1,0:T(8,128)} %bitcast.11), custom_call_target="tpu_custom_call" | custom-call | tf_op jit(solution)/shard_map/deposit/pallas_call | solution.py:422
  8.2 0.0 copy-done.2
  8.3 0.0 copy-start
  8.3 1.2 %copy-done = f32[4,520,128]{2,1,0:T(8,128)S(1)} copy-done((f32[4,520,128]{2,1,0:T(8,128)S(1)}, f32[4,520,128]{2,1,0:T(8,128)}, u32[]{:S(2)}) %copy-start) | copy-done | bytes 1064984
  9.5 0.0 copy-start.1
  9.5 0.7 copy-done.1
  10.2 60.8 %world.1 = (f32[8,64,128]{2,1,0:T(8,128)S(1)}, f32[1,8,64,128]{3,2,1,0:T(8,128)S(1)}) custom-call(f32[3]{0:T(128)S(1)} %bitcast.10, f32[4,520,128]{2,1,0:T(8,128)S(1)} %copy-done, f32[32,128]{1,0:T(8,128)S(1)} %copy-done.1), custom_call_target="tpu_custom_call" | custom-call | tf_op jit(solution)/shard_map/world/pallas_call | solution.py:440
  71.0 0.7 copy.14
  71.7 0.7 copy.15
Async XLA Ops:
  0.6 7.6 %copy-start.2 = (f32[1,3]{1,0:T(1,128)S(1)}, f32[1,3]{1,0:T(1,128)}, u32[]{:S(2)}) copy-start(f32[1,3]{1,0:T(1,128)} %param.10) | copy-start | bytes 40
  8.3 1.2 %copy-start = (f32[4,520,128]{2,1,0:T(8,128)S(1)}, f32[4,520,128]{2,1,0:T(8,128)}, u32[]{:S(2)}) copy-start(f32[4,520,128]{2,1,0:T(8,128)} %get-tuple-element.4.acc_ref) | copy-start | bytes 3194884
  9.5 0.7 copy-start.1

commit v2 on v1

--- a/solution.py
+++ b/solution.py
@@ -13,51 +13,67 @@
 CHUNK = 4
 
 DATA_FLOOR = 0.25
-PRECISE = lax.Precision.HIGHEST
 MESH = pl.DeviceIdType.MESH
 
 
-def deposit_kernel(rows, dest, offs, level, frac, psf, cam_ref, acc_ref, tap_ref):
-    step = pl.program_id(0)
-    taps = psf.shape[1]
-
-    @pl.when(step == 0)
-    def _():
-        @pl.loop(0, acc_ref.shape[0])
-        def _(s):
-            acc_ref[s] = jnp.zeros(acc_ref.shape[1:], jnp.float32)
-
-        tap_ref[...] = jnp.zeros(tap_ref.shape, jnp.float32)
-        for axis in range(3):
-            scale = psf[axis, 0]
-            for t in range(1, taps):
-                scale = scale + psf[axis, t]
-            scale = jnp.full((1, 128), scale, jnp.float32)
-            for t in range(taps):
-                at = axis * taps + t
-                tap_ref[at : at + 1, :] = jnp.full((1, 128), psf[axis, t], jnp.float32) / scale
+def deposit_kernel(
+    rows, dest_ref, offs_ref, level_ref, frac_ref, psf_ref, cam_ref, acc_ref, tap_ref,
+    dest, offs, level, frac, psf, cam, sems, small_sems,
+):
+    taps = psf_ref.shape[2]
+    blocks, planes = cam_ref.shape[:2]
+
+    def fetch(c):
+        at = pl.ds(c * CHUNK, CHUNK)
+        return pltpu.make_async_copy(cam_ref.at[at], cam.at[at], sems.at[c])
+
+    small = [pltpu.make_async_copy(a, b, small_sems.at[n]) for n, (a, b) in enumerate(
+        [(dest_ref, dest), (offs_ref, offs), (level_ref, level), (frac_ref, frac), (psf_ref, psf)])]
+    for copy in small:
+        copy.start()
+    for c in range(blocks // CHUNK):
+        fetch(c).start()
+
+    @pl.loop(0, acc_ref.shape[0])
+    def _(s):
+        acc_ref[s] = jnp.zeros(acc_ref.shape[1:], jnp.float32)
+
+    for copy in small:
+        copy.wait()
+
+    tap_ref[...] = jnp.zeros(tap_ref.shape, jnp.float32)
+    for axis in range(3):
+        scale = jnp.sum(psf[axis], axis=1, keepdims=True)
+        share = psf[axis] / scale
+        for t in range(taps):
+            at = axis * taps + t
+            tap_ref[at : at + 1, :] = jnp.broadcast_to(share[:, t : t + 1], (1, 128))
 
     fz = frac[0]
     base = level[0].astype(jnp.float32)
-    for i in range(cam_ref.shape[0]):
-        b = step * cam_ref.shape[0] + i
-        s = dest[b]
-        o = offs[b]
-        lower = cam_ref[i, 0] - base
-        for k in range(cam_ref.shape[1] - 1):
-            upper = cam_ref[i, k + 1] - base
-            at = pl.ds(pl.multiple_of((o + k) * rows, 8), rows)
-            acc_ref[s, at, :] = acc_ref[s, at, :] + ((1.0 - fz) * lower + fz * upper)
-            cnt = pl.ds(CZ * rows + o + k, 1)
-            acc_ref[s, cnt, :] = acc_ref[s, cnt, :] + 1.0
-            lower = upper
+
+    @pl.loop(0, blocks // CHUNK)
+    def _(c):
+        fetch(c).wait()
+        for i in range(CHUNK):
+            b = c * CHUNK + i
+            s = dest[b]
+            o = offs[b]
+            lower = cam[b, 0] - base
+            for k in range(planes - 1):
+                upper = cam[b, k + 1] - base
+                at = pl.ds(pl.multiple_of((o + k) * rows, 8), rows)
+                acc_ref[s, at, :] = acc_ref[s, at, :] + ((1.0 - fz) * lower + fz * upper)
+                cnt = pl.ds(CZ * rows + o + k, 1)
+                acc_ref[s, cnt, :] = acc_ref[s, cnt, :] + 1.0
+                lower = upper
 
 
 def world_kernel(
     dims, rows, taps,
-    frac, acc_ref, tap_in, est_ref, joined_ref,
-    recv, tap_all, jx, e0, e1, kx, za, zb, rt, yb, lg,
-    a2a_s, a2a_r, own_sem, tap_s, tap_r, row_s, row_r, lo_s, lo_r, hi_s, hi_r, loc_sem,
+    frac_ref, acc_ref, tap_in, est_ref, joined_ref,
+    frac, up_in, down_in, tap_all, jx, e0, e1, kx, za, zb, rt, yb, lg,
+    up_s, up_r, down_s, down_r, frac_sem, tap_s, tap_r, row_s, row_r, lo_s, lo_r, hi_s, hi_r, loc_sem,
     zs, zr, es, er, out_s, out_r,
 ):
     slabs, views, bands = dims
@@ -85,6 +101,9 @@
     below, above = z > 0, z < slabs - 1
     left, right = me > 0, me < strips - 1
 
+    own_frac = pltpu.make_async_copy(frac_ref, frac, frac_sem)
+    own_frac.start()
+
     @pl.loop(0, views)
     def _(w):
         @pl.loop(0, 3 * CZ)
@@ -100,15 +119,18 @@
     def greet(target):
         pl.semaphore_signal(barrier, inc=1, device_id=target, device_id_type=MESH)
 
-    for d in range(1, slabs):
-        greet(dev((z + d) % slabs, v, g))
+    for ok, dz in ((below, -1), (above, 1)):
+        @pl.when(ok)
+        def _(dz=dz):
+            greet(dev(z + dz, v, g))
+
     for d in range(1, strips):
         greet(strip_dev(z, (me + d) % strips))
     corners = []
     for dz, zok in ((-1, below), (1, above)):
         for ds, sok in ((-1, left), (1, right)):
             corners.append((dz, ds, zok & sok))
-    amount = slabs - 1 + strips - 1
+    amount = strips - 1 + below.astype(jnp.int32) + above.astype(jnp.int32)
     for dz, ds, ok in corners:
         amount = amount + ok.astype(jnp.int32)
 
@@ -118,16 +140,21 @@
 
     pl.semaphore_wait(barrier, amount)
 
-    def a2a(d):
-        to = (z + d) % slabs
-        return pltpu.make_async_remote_copy(
-            src_ref=acc_ref.at[to], dst_ref=recv.at[d - 1], send_sem=a2a_s.at[d - 1],
-            recv_sem=a2a_r.at[d - 1], device_id=dev(to, v, g), device_id_type=MESH)
-
-    for d in range(1, slabs):
-        a2a(d).start()
-    own = pltpu.make_async_copy(acc_ref.at[z], recv.at[slabs - 1], own_sem)
-    own.start()
+    def relay(up, s, own):
+        buf, sems = (up_in, (up_s, up_r)) if up else (down_in, (down_s, down_r))
+        return pltpu.make_async_remote_copy(
+            src_ref=acc_ref.at[s] if own else buf.at[s], dst_ref=buf.at[s], send_sem=sems[0].at[s],
+            recv_sem=sems[1].at[s], device_id={"gz": z + 1 if up else z - 1}, device_id_type=MESH)
+
+    ends = ((True, below, lambda s: z < s), (False, above, lambda s: z > s))
+    up_order, down_order = list(range(slabs - 1, 0, -1)), list(range(slabs - 1))
+
+    for s_up, s_down in zip(up_order, down_order):
+        for (up, inner_device, passes), s in zip(ends, (s_up, s_down)):
+            @pl.when(passes(s) & jnp.logical_not(inner_device))
+            def _(up=up, s=s):
+                relay(up, s, True).start()
+
     own_tap = pltpu.make_async_copy(tap_in, tap_all.at[v], loc_sem.at[1])
     own_tap.start()
 
@@ -152,13 +179,31 @@
             tap = tap_all[w, 2 * taps + t : 2 * taps + t + 1, :]
             ahead = jnp.where(apart == t - margin, tap, ahead)
             back = jnp.where(apart == margin - t, tap, back)
-        kx[w, 0] = ahead
-        kx[w, 1] = back
-
-    own.wait()
-    for d in range(1, slabs):
-        a2a(d).wait_recv()
-
+        for n, full in enumerate((ahead, back)):
+            top = full.astype(jnp.bfloat16)
+            kx[w, n, 0:128, 0:128] = top
+            kx[w, n, 128:256, 0:128] = top
+            kx[w, n, 0:128, 128:256] = (full - top.astype(jnp.float32)).astype(jnp.bfloat16)
+            kx[w, n, 128:256, 128:256] = jnp.zeros((128, 128), jnp.bfloat16)
+
+    for s_up, s_down in zip(up_order, down_order):
+        for (up, inner_device, passes), s in zip(ends, (s_up, s_down)):
+            @pl.when(passes(s) & inner_device)
+            def _(up=up, s=s):
+                buf = up_in if up else down_in
+                relay(up, s, False).wait_recv()
+                buf[s] = buf[s] + acc_ref[s]
+                relay(up, s, False).start()
+
+    @pl.when(below)
+    def _():
+        relay(True, z, False).wait_recv()
+
+    @pl.when(above)
+    def _():
+        relay(False, z, False).wait_recv()
+
+    own_frac.wait()
     fy, fx = frac[1], frac[2]
     last_row = lax.broadcasted_iota(jnp.int32, (rows, 128), 0) == rows - 1
     last_col = lax.broadcasted_iota(jnp.int32, (rows, 128), 1) == 127
@@ -167,11 +212,11 @@
     def _(p):
         at = pl.ds(pl.multiple_of(p * rows, 8), rows)
         cnt = pl.ds(CZ * rows + p, 1)
-        total = recv[0, at, :]
-        covered = recv[0, cnt, :]
-        for s in range(1, slabs):
-            total = total + recv[s, at, :]
-            covered = covered + recv[s, cnt, :]
+        total = acc_ref[z, at, :]
+        covered = acc_ref[z, cnt, :]
+        for ok, buf in ((below, up_in), (above, down_in)):
+            total = total + jnp.where(ok, buf[z, at, :], 0.0)
+            covered = covered + jnp.where(ok, buf[z, cnt, :], 0.0)
         follow = jnp.where(last_row, total, pltpu.roll(total, rows - 1, 0))
         total = (1.0 - fy) * total + fy * follow
         follow = jnp.where(last_col, total, pltpu.roll(total, 127, 1))
@@ -285,50 +330,60 @@
     planes_r = CZ + 2 * margin
     rows_r = strip + 2 * margin
 
+    def along_x(u, w, n):
+        top = u.astype(jnp.bfloat16)
+        rest = (u - top.astype(jnp.float32)).astype(jnp.bfloat16)
+        both = jnp.dot(jnp.concatenate([top, rest], axis=1), kx[w, n], preferred_element_type=jnp.float32)
+        return both[:, 0:128] + both[:, 128:256]
+
+    def weighted(terms, weights):
+        total = weights[0] * terms[0]
+        for term, weight in zip(terms[1:], weights[1:]):
+            total = total + weight * term
+        return total
+
     def correct(est):
         for w in range(views):
             def tap(axis, t):
                 at = axis * taps + t
                 return tap_all[w, at : at + 1, :]
 
-            @pl.loop(0, planes_r)
+            @pl.loop(0, wide // 8, unroll=2)
+            def _(r):
+                at = pl.ds(pl.multiple_of(r * 8, 8), 8)
+                column = [est[CZ - 2 * margin + p, at, :] for p in range(planes_r + 2 * margin)]
+                for p in range(planes_r):
+                    za[p, at, :] = weighted(column[p : p + taps], [tap(0, t) for t in range(taps)])
+
+            @pl.loop(0, planes_r, unroll=4)
             def _(p):
-                total = tap(0, 0) * est[p + CZ - 2 * margin]
-                for t in range(1, taps):
-                    total = total + tap(0, t) * est[p + CZ - 2 * margin + t]
-                za[p] = total
                 base = HALO - 2 * margin
-                total = tap(1, 0) * za[p, base : base + rows_r, :]
-                for t in range(1, taps):
-                    total = total + tap(1, t) * za[p, base + t : base + t + rows_r, :]
-                zb[p] = total
+                zb[p] = weighted([za[p, base + t : base + t + rows_r, :] for t in range(taps)],
+                                 [tap(1, t) for t in range(taps)])
 
             @pl.loop(0, planes_r // 4)
             def _(c):
                 at = pl.ds(c * 4, 4)
-                blurred = jnp.dot(
-                    zb[at].reshape(4 * rows_r, 128), kx[w, 0], precision=PRECISE,
-                    preferred_element_type=jnp.float32).reshape(4, rows_r, 128)
+                blurred = along_x(zb[at].reshape(4 * rows_r, 128), w, 0).reshape(4, rows_r, 128)
                 data = jx[w, pl.ds(c * 4 + CZ - margin, 4), HALO - margin : HALO - margin + rows_r, :]
                 rt[at] = jnp.where(data > 0.0, data / blurred, 0.0)
 
-            @pl.loop(0, CZ)
+            @pl.loop(0, rows_r // 8, unroll=True)
+            def _(r):
+                at = pl.ds(pl.multiple_of(r * 8, 8), 8)
+                column = [rt[p, at, :] for p in range(planes_r)]
+                for p in range(CZ):
+                    za[p, at, :] = weighted(column[p : p + taps], [tap(0, taps - 1 - t) for t in range(taps)])
+
+            @pl.loop(0, CZ, unroll=4)
             def _(p):
-                total = tap(0, taps - 1) * rt[p]
-                for t in range(1, taps):
-                    total = total + tap(0, taps - 1 - t) * rt[p + t]
-                za[p, 0:rows_r, :] = total
-                total = tap(1, taps - 1) * za[p, 0:strip, :]
-                for t in range(1, taps):
-                    total = total + tap(1, taps - 1 - t) * za[p, t : t + strip, :]
-                yb[p] = total
+                yb[p] = weighted([za[p, t : t + strip, :] for t in range(taps)],
+                                 [tap(1, taps - 1 - t) for t in range(taps)])
 
             @pl.loop(0, CZ // 4)
             def _(c):
                 at = pl.ds(c * 4, 4)
-                logs = jnp.log(jnp.dot(
-                    yb[at].reshape(4 * strip, 128), kx[w, 1], precision=PRECISE,
-                    preferred_element_type=jnp.float32)).reshape(4, strip, 128)
+                logs = jnp.log(along_x(yb[at].reshape(4 * strip, 128), w, 1)).reshape(4, strip, 128)
                 lg[at] = logs if w == 0 else lg[at] + logs
 
     inner = pl.ds(HALO, strip)
@@ -377,8 +432,12 @@
     for d in range(1, views):
         out_copy((v + d) % views, d - 1).wait()
 
-    for d in range(1, slabs):
-        a2a(d).wait_send()
+    for s_up, s_down in zip(up_order, down_order):
+        for (up, _, passes), s in zip(ends, (s_up, s_down)):
+            @pl.when(passes(s))
+            def _(up=up, s=s):
+                relay(up, s, False).wait_send()
+
     for i in range(views):
         owner = snake(g, i)
 
@@ -418,51 +477,60 @@
     strip = rows // views
     wide = strip + 2 * HALO
     tap_rows = -(-3 * taps // 8) * 8
-    smem = pl.BlockSpec(memory_space=pltpu.SMEM)
+    vmem = pl.BlockSpec(memory_space=pltpu.VMEM)
+    hbm = pl.BlockSpec(memory_space=pltpu.HBM)
     acc, tap_rows_all = pl.pallas_call(
         functools.partial(deposit_kernel, rows),
-        grid=(blocks // CHUNK,),
-        in_specs=[smem] * 5 + [pl.BlockSpec((CHUNK, planes, rows, cols), lambda i: (i, 0, 0, 0))],
-        out_specs=(
-            pl.BlockSpec((slabs, tall, cols), lambda i: (0, 0, 0)),
-            pl.BlockSpec((tap_rows, cols), lambda i: (0, 0)),
-        ),
+        in_specs=[hbm] * 6,
+        out_specs=(vmem, vmem),
         out_shape=(
             jax.ShapeDtypeStruct((slabs, tall, cols), jnp.float32),
             jax.ShapeDtypeStruct((tap_rows, cols), jnp.float32),
         ),
+        scratch_shapes=[
+            pltpu.SMEM((blocks,), jnp.int32),
+            pltpu.SMEM((blocks,), jnp.int32),
+            pltpu.SMEM((1,), jnp.int32),
+            pltpu.SMEM((3,), jnp.float32),
+            pltpu.VMEM((3, 1, taps), jnp.float32),
+            pltpu.VMEM((blocks, planes, rows, cols), jnp.float32),
+            pltpu.SemaphoreType.DMA((blocks // CHUNK,)),
+            pltpu.SemaphoreType.DMA((5,)),
+        ],
+        compiler_params=pltpu.CompilerParams(vmem_limit_bytes=60 * 1024 * 1024),
         name="deposit",
-    )(destination.reshape(-1), offsets.reshape(-1), background.reshape(-1), shift_frac[0], psf_taps[0], camera[0])
-
-    vmem = pl.BlockSpec(memory_space=pltpu.VMEM)
+    )(destination.reshape(-1), offsets.reshape(-1), background.reshape(-1), shift_frac[0], jnp.transpose(psf_taps, (1, 0, 2)), camera[0])
+
     dma = pltpu.SemaphoreType.DMA
     f32 = jnp.float32
     estimate, joined = pl.pallas_call(
         functools.partial(world_kernel, dims, rows, taps),
-        in_specs=[smem, pl.BlockSpec(memory_space=pl.ANY), vmem],
+        in_specs=[hbm, vmem, vmem],
         out_specs=(vmem, vmem),
         out_shape=(
             jax.ShapeDtypeStruct((CZ, rows, cols), f32),
             jax.ShapeDtypeStruct((1, CZ, rows, cols), f32),
         ),
         scratch_shapes=[
+            pltpu.SMEM((3,), f32),
+            pltpu.VMEM((slabs, tall, cols), f32),
             pltpu.VMEM((slabs, tall, cols), f32),
             pltpu.VMEM((views, tap_rows, cols), f32),
             pltpu.VMEM((views, 3 * CZ, wide, cols), f32),
             pltpu.VMEM((3 * CZ, wide, cols), f32),
             pltpu.VMEM((3 * CZ, wide, cols), f32),
-            pltpu.VMEM((views, 2, cols, cols), f32),
+            pltpu.VMEM((views, 2, 2 * cols, 2 * cols), jnp.bfloat16),
             pltpu.VMEM((CZ + 2 * margin, wide, cols), f32),
             pltpu.VMEM((CZ + 2 * margin, strip + 2 * margin, cols), f32),
             pltpu.VMEM((CZ + 2 * margin, strip + 2 * margin, cols), f32),
             pltpu.VMEM((CZ, strip, cols), f32),
             pltpu.VMEM((CZ, strip, cols), f32),
-            dma((slabs,)), dma((slabs,)), dma, dma((views,)), dma((views,)),
+            dma((slabs,)), dma((slabs,)), dma((slabs,)), dma((slabs,)), dma, dma((views,)), dma((views,)),
             dma((views,)), dma((views,)), dma, dma((views,)), dma, dma((views,)), dma((2,)),
             dma((2, views)), dma((2, views)), dma((8,)), dma((8,)), dma((views,)), dma((views,)),
         ],
         compiler_params=pltpu.CompilerParams(
-            collective_id=0, has_side_effects=True, vmem_limit_bytes=40 * 1024 * 1024),
+            collective_id=0, has_side_effects=True, vmem_limit_bytes=58 * 1024 * 1024),
         name="world",
     )(shift_frac[0], acc, tap_rows_all)
     return estimate, joined

time: 72.7 us -> 73.4 us (level)
  the two profiles are of different devices: /device:TPU:8 before, /device:TPU:0 now
where the time goes in v2:
time: 73.4 us; the launch traced here: 73.2 us
  Pallas kernels  68.6 us (93%)
  local copies, waits for them, and re-layouts  3.34 us (5%)
  between operations  1.29 us (2%)
    pallas_call x1, Pallas kernels, on_device(): pl.pallas_call(functools.partial(world_kernel, dims, rows, taps), in_spec...  65.2 us
    pallas_call x1, Pallas kernels, on_device(): pl.pallas_call(functools.partial(deposit_kernel, rows), in_specs=[hbm] *...  3.42 us
    unnamed x2, local copies, waits for them, and re-layouts  3.34 us

profile of v2, /device:TPU:0, one launch (start us, length us, event | category | flops | bytes accessed | tf_op | source)
XLA Modules:
  0.0 73.2 jit_solution(16000341622421067944)
XLA Ops:
  1.3 3.4 %deposit.1 = (f32[4,520,128]{2,1,0:T(8,128)}, f32[32,128]{1,0:T(8,128)}) custom-call(s32[32]{0:T(128)} %bitcast.11, s32[32]{0:T(128)} %bitcast.12, s32[1]{0:T(128)} %bitcast.6.level_ref, f32[3]{0:T(128)} %bitcast.8, f32[3,1,9]{2,1,0:T(1,128)} %bitcast.10, f32[32,3,64,128]{3,2,1,0:T(8,128)} %bitcast.7), custom_call_target="tpu_custom_call" | custom-call | tf_op jit(solution)/shard_map/deposit/pallas_call | solution.py:482
  4.7 65.2 %world.1 = (f32[8,64,128]{2,1,0:T(8,128)}, f32[1,8,64,128]{3,2,1,0:T(8,128)}) custom-call(f32[3]{0:T(128)} %bitcast.9, f32[4,520,128]{2,1,0:T(8,128)} %get-tuple-element.4.acc_ref, f32[32,128]{1,0:T(8,128)} %get-tuple-element.5.tap_in), custom_call_target="tpu_custom_call" | custom-call | tf_op jit(solution)/shard_map/world/pallas_call | solution.py:506
  69.9 1.7 %copy.11 = f32[8,64,128]{2,1,0:T(8,128)} copy(f32[8,64,128]{2,1,0:T(8,128)} %get-tuple-element.8) | data formatting | bytes 524288
  71.5 1.7 %copy.12 = f32[1,8,64,128]{3,2,1,0:T(8,128)} copy(f32[1,8,64,128]{3,2,1,0:T(8,128)} %get-tuple-element.9) | data formatting | bytes 524288

commit v3 on v2

--- a/solution.py
+++ b/solution.py
@@ -16,30 +16,20 @@
 MESH = pl.DeviceIdType.MESH
 
 
-def deposit_kernel(
-    rows, dest_ref, offs_ref, level_ref, frac_ref, psf_ref, cam_ref, acc_ref, tap_ref,
-    dest, offs, level, frac, psf, cam, sems, small_sems,
-):
-    taps = psf_ref.shape[2]
+def deposit_kernel(rows, dest, offs, level, frac, psf, cam_ref, acc_ref, tap_ref, cam, sems):
+    taps = psf.shape[2]
     blocks, planes = cam_ref.shape[:2]
 
     def fetch(c):
         at = pl.ds(c * CHUNK, CHUNK)
         return pltpu.make_async_copy(cam_ref.at[at], cam.at[at], sems.at[c])
 
-    small = [pltpu.make_async_copy(a, b, small_sems.at[n]) for n, (a, b) in enumerate(
-        [(dest_ref, dest), (offs_ref, offs), (level_ref, level), (frac_ref, frac), (psf_ref, psf)])]
-    for copy in small:
-        copy.start()
     for c in range(blocks // CHUNK):
         fetch(c).start()
 
     @pl.loop(0, acc_ref.shape[0])
     def _(s):
         acc_ref[s] = jnp.zeros(acc_ref.shape[1:], jnp.float32)
-
-    for copy in small:
-        copy.wait()
 
     tap_ref[...] = jnp.zeros(tap_ref.shape, jnp.float32)
     for axis in range(3):
@@ -71,9 +61,9 @@
 
 def world_kernel(
     dims, rows, taps,
-    frac_ref, acc_ref, tap_in, est_ref, joined_ref,
-    frac, up_in, down_in, tap_all, jx, e0, e1, kx, za, zb, rt, yb, lg,
-    up_s, up_r, down_s, down_r, frac_sem, tap_s, tap_r, row_s, row_r, lo_s, lo_r, hi_s, hi_r, loc_sem,
+    frac, acc_ref, tap_in, est_ref, joined_ref,
+    recv, tap_all, jx, e0, e1, kx, za, zb, rt, yb, lg,
+    a2a_s, a2a_r, own_sem, tap_s, tap_r, row_s, row_r, lo_s, lo_r, hi_s, hi_r, loc_sem,
     zs, zr, es, er, out_s, out_r,
 ):
     slabs, views, bands = dims
@@ -101,9 +91,6 @@
     below, above = z > 0, z < slabs - 1
     left, right = me > 0, me < strips - 1
 
-    own_frac = pltpu.make_async_copy(frac_ref, frac, frac_sem)
-    own_frac.start()
-
     @pl.loop(0, views)
     def _(w):
         @pl.loop(0, 3 * CZ)
@@ -119,18 +106,15 @@
     def greet(target):
         pl.semaphore_signal(barrier, inc=1, device_id=target, device_id_type=MESH)
 
-    for ok, dz in ((below, -1), (above, 1)):
-        @pl.when(ok)
-        def _(dz=dz):
-            greet(dev(z + dz, v, g))
-
+    for d in range(1, slabs):
+        greet(dev((z + d) % slabs, v, g))
     for d in range(1, strips):
         greet(strip_dev(z, (me + d) % strips))
     corners = []
     for dz, zok in ((-1, below), (1, above)):
         for ds, sok in ((-1, left), (1, right)):
             corners.append((dz, ds, zok & sok))
-    amount = strips - 1 + below.astype(jnp.int32) + above.astype(jnp.int32)
+    amount = slabs - 1 + strips - 1
     for dz, ds, ok in corners:
         amount = amount + ok.astype(jnp.int32)
 
@@ -140,21 +124,16 @@
 
     pl.semaphore_wait(barrier, amount)
 
-    def relay(up, s, own):
-        buf, sems = (up_in, (up_s, up_r)) if up else (down_in, (down_s, down_r))
-        return pltpu.make_async_remote_copy(
-            src_ref=acc_ref.at[s] if own else buf.at[s], dst_ref=buf.at[s], send_sem=sems[0].at[s],
-            recv_sem=sems[1].at[s], device_id={"gz": z + 1 if up else z - 1}, device_id_type=MESH)
-
-    ends = ((True, below, lambda s: z < s), (False, above, lambda s: z > s))
-    up_order, down_order = list(range(slabs - 1, 0, -1)), list(range(slabs - 1))
-
-    for s_up, s_down in zip(up_order, down_order):
-        for (up, inner_device, passes), s in zip(ends, (s_up, s_down)):
-            @pl.when(passes(s) & jnp.logical_not(inner_device))
-            def _(up=up, s=s):
-                relay(up, s, True).start()
-
+    def a2a(d):
+        to = (z + d) % slabs
+        return pltpu.make_async_remote_copy(
+            src_ref=acc_ref.at[to], dst_ref=recv.at[d - 1], send_sem=a2a_s.at[d - 1],
+            recv_sem=a2a_r.at[d - 1], device_id=dev(to, v, g), device_id_type=MESH)
+
+    for d in range(1, slabs):
+        a2a(d).start()
+    own = pltpu.make_async_copy(acc_ref.at[z], recv.at[slabs - 1], own_sem)
+    own.start()
     own_tap = pltpu.make_async_copy(tap_in, tap_all.at[v], loc_sem.at[1])
     own_tap.start()
 
@@ -186,24 +165,10 @@
             kx[w, n, 0:128, 128:256] = (full - top.astype(jnp.float32)).astype(jnp.bfloat16)
             kx[w, n, 128:256, 128:256] = jnp.zeros((128, 128), jnp.bfloat16)
 
-    for s_up, s_down in zip(up_order, down_order):
-        for (up, inner_device, passes), s in zip(ends, (s_up, s_down)):
-            @pl.when(passes(s) & inner_device)
-            def _(up=up, s=s):
-                buf = up_in if up else down_in
-                relay(up, s, False).wait_recv()
-                buf[s] = buf[s] + acc_ref[s]
-                relay(up, s, False).start()
-
-    @pl.when(below)
-    def _():
-        relay(True, z, False).wait_recv()
-
-    @pl.when(above)
-    def _():
-        relay(False, z, False).wait_recv()
-
-    own_frac.wait()
+    own.wait()
+    for d in range(1, slabs):
+        a2a(d).wait_recv()
+
     fy, fx = frac[1], frac[2]
     last_row = lax.broadcasted_iota(jnp.int32, (rows, 128), 0) == rows - 1
     last_col = lax.broadcasted_iota(jnp.int32, (rows, 128), 1) == 127
@@ -212,11 +177,11 @@
     def _(p):
         at = pl.ds(pl.multiple_of(p * rows, 8), rows)
         cnt = pl.ds(CZ * rows + p, 1)
-        total = acc_ref[z, at, :]
-        covered = acc_ref[z, cnt, :]
-        for ok, buf in ((below, up_in), (above, down_in)):
-            total = total + jnp.where(ok, buf[z, at, :], 0.0)
-            covered = covered + jnp.where(ok, buf[z, cnt, :], 0.0)
+        total = recv[0, at, :]
+        covered = recv[0, cnt, :]
+        for s in range(1, slabs):
+            total = total + recv[s, at, :]
+            covered = covered + recv[s, cnt, :]
         follow = jnp.where(last_row, total, pltpu.roll(total, rows - 1, 0))
         total = (1.0 - fy) * total + fy * follow
         follow = jnp.where(last_col, total, pltpu.roll(total, 127, 1))
@@ -432,12 +397,8 @@
     for d in range(1, views):
         out_copy((v + d) % views, d - 1).wait()
 
-    for s_up, s_down in zip(up_order, down_order):
-        for (up, _, passes), s in zip(ends, (s_up, s_down)):
-            @pl.when(passes(s))
-            def _(up=up, s=s):
-                relay(up, s, False).wait_send()
-
+    for d in range(1, slabs):
+        a2a(d).wait_send()
     for i in range(views):
         owner = snake(g, i)
 
@@ -477,25 +438,19 @@
     strip = rows // views
     wide = strip + 2 * HALO
     tap_rows = -(-3 * taps // 8) * 8
+    smem = pl.BlockSpec(memory_space=pltpu.SMEM)
     vmem = pl.BlockSpec(memory_space=pltpu.VMEM)
-    hbm = pl.BlockSpec(memory_space=pltpu.HBM)
     acc, tap_rows_all = pl.pallas_call(
         functools.partial(deposit_kernel, rows),
-        in_specs=[hbm] * 6,
+        in_specs=[smem] * 4 + [vmem, pl.BlockSpec(memory_space=pl.ANY)],
         out_specs=(vmem, vmem),
         out_shape=(
             jax.ShapeDtypeStruct((slabs, tall, cols), jnp.float32),
             jax.ShapeDtypeStruct((tap_rows, cols), jnp.float32),
         ),
         scratch_shapes=[
-            pltpu.SMEM((blocks,), jnp.int32),
-            pltpu.SMEM((blocks,), jnp.int32),
-            pltpu.SMEM((1,), jnp.int32),
-            pltpu.SMEM((3,), jnp.float32),
-            pltpu.VMEM((3, 1, taps), jnp.float32),
             pltpu.VMEM((blocks, planes, rows, cols), jnp.float32),
             pltpu.SemaphoreType.DMA((blocks // CHUNK,)),
-            pltpu.SemaphoreType.DMA((5,)),
         ],
         compiler_params=pltpu.CompilerParams(vmem_limit_bytes=60 * 1024 * 1024),
         name="deposit",
@@ -505,15 +460,13 @@
     f32 = jnp.float32
     estimate, joined = pl.pallas_call(
         functools.partial(world_kernel, dims, rows, taps),
-        in_specs=[hbm, vmem, vmem],
+        in_specs=[smem, vmem, vmem],
         out_specs=(vmem, vmem),
         out_shape=(
             jax.ShapeDtypeStruct((CZ, rows, cols), f32),
             jax.ShapeDtypeStruct((1, CZ, rows, cols), f32),
         ),
         scratch_shapes=[
-            pltpu.SMEM((3,), f32),
-            pltpu.VMEM((slabs, tall, cols), f32),
             pltpu.VMEM((slabs, tall, cols), f32),
             pltpu.VMEM((views, tap_rows, cols), f32),
             pltpu.VMEM((views, 3 * CZ, wide, cols), f32),
@@ -525,12 +478,12 @@
             pltpu.VMEM((CZ + 2 * margin, strip + 2 * margin, cols), f32),
             pltpu.VMEM((CZ, strip, cols), f32),
             pltpu.VMEM((CZ, strip, cols), f32),
-            dma((slabs,)), dma((slabs,)), dma((slabs,)), dma((slabs,)), dma, dma((views,)), dma((views,)),
+            dma((slabs,)), dma((slabs,)), dma, dma((views,)), dma((views,)),
             dma((views,)), dma((views,)), dma, dma((views,)), dma, dma((views,)), dma((2,)),
             dma((2, views)), dma((2, views)), dma((8,)), dma((8,)), dma((views,)), dma((views,)),
         ],
         compiler_params=pltpu.CompilerParams(
-            collective_id=0, has_side_effects=True, vmem_limit_bytes=58 * 1024 * 1024),
+            collective_id=0, has_side_effects=True, vmem_limit_bytes=40 * 1024 * 1024),
         name="world",
     )(shift_frac[0], acc, tap_rows_all)
     return estimate, joined

time: 73.4 us -> 67.8 us (0.924)
  the two profiles are of different devices: /device:TPU:0 before, /device:TPU:8 now
where the time goes in v3:
time: 67.8 us; the launch traced here: 67.5 us
  Pallas kernels  62.8 us (93%)
  local copies, waits for them, and re-layouts  3.35 us (5%)
  between operations  1.33 us (2%)
    pallas_call x1, Pallas kernels, on_device(): pl.pallas_call(functools.partial(world_kernel, dims, rows, taps), in_spec...  59.2 us
    pallas_call x1, Pallas kernels, on_device(): pl.pallas_call(functools.partial(deposit_kernel, rows), in_specs=[smem] *...  3.65 us
    unnamed x8, local copies, waits for them, and re-layouts  3.35 us

profile of v3, /device:TPU:8, one launch (start us, length us, event | category | flops | bytes accessed | tf_op | source)
XLA Modules:
  0.0 67.5 jit_solution(4908452163243005752)
XLA Ops:
  0.6 0.0 copy-start.2
  1.3 3.6 %deposit.1 = (f32[4,520,128]{2,1,0:T(8,128)}, f32[32,128]{1,0:T(8,128)}) custom-call(s32[32]{0:T(128)} %bitcast.11, s32[32]{0:T(128)} %bitcast.12, s32[1]{0:T(128)} %bitcast.6.level, f32[3]{0:T(128)} %bitcast.7, f32[3,1,9]{2,1,0:T(1,128)} %bitcast.10, f32[32,3,64,128]{3,2,1,0:T(8,128)} %bitcast.9), custom_call_target="tpu_custom_call" | custom-call | tf_op jit(solution)/shard_map/deposit/pallas_call | solution.py:443
  5.0 0.0 copy-done.2
  5.0 0.0 copy-start
  5.0 1.2 %copy-done = f32[4,520,128]{2,1,0:T(8,128)S(1)} copy-done((f32[4,520,128]{2,1,0:T(8,128)S(1)}, f32[4,520,128]{2,1,0:T(8,128)}, u32[]{:S(2)}) %copy-start) | copy-done | bytes 1064984
  6.2 0.0 copy-start.1
  6.2 0.7 %copy-done.1 = f32[32,128]{1,0:T(8,128)S(1)} copy-done((f32[32,128]{1,0:T(8,128)S(1)}, f32[32,128]{1,0:T(8,128)}, u32[]{:S(2)}) %copy-start.1) | copy-done | bytes 16408
  6.9 59.2 %world.1 = (f32[8,64,128]{2,1,0:T(8,128)S(1)}, f32[1,8,64,128]{3,2,1,0:T(8,128)S(1)}) custom-call(f32[3]{0:T(128)S(1)} %bitcast.8, f32[4,520,128]{2,1,0:T(8,128)S(1)} %copy-done, f32[32,128]{1,0:T(8,128)S(1)} %copy-done.1), custom_call_target="tpu_custom_call" | custom-call | tf_op jit(solution)/shard_map/world/pallas_call | solution.py:461
  66.1 0.7 %copy.11 = f32[8,64,128]{2,1,0:T(8,128)} copy(f32[8,64,128]{2,1,0:T(8,128)S(1)} %get-tuple-element.8) | data formatting | bytes 524288
  66.8 0.7 %copy.12 = f32[1,8,64,128]{3,2,1,0:T(8,128)} copy(f32[1,8,64,128]{3,2,1,0:T(8,128)S(1)} %get-tuple-element.9) | data formatting | bytes 524288
Async XLA Ops:
  0.6 4.3 %copy-start.2 = (f32[1,3]{1,0:T(1,128)S(1)}, f32[1,3]{1,0:T(1,128)}, u32[]{:S(2)}) copy-start(f32[1,3]{1,0:T(1,128)} %param.10) | copy-start | bytes 40
  5.0 1.2 %copy-start = (f32[4,520,128]{2,1,0:T(8,128)S(1)}, f32[4,520,128]{2,1,0:T(8,128)}, u32[]{:S(2)}) copy-start(f32[4,520,128]{2,1,0:T(8,128)} %get-tuple-element.4.acc_ref) | copy-start | bytes 3194884
  6.2 0.7 %copy-start.1 = (f32[32,128]{1,0:T(8,128)S(1)}, f32[32,128]{1,0:T(8,128)}, u32[]{:S(2)}) copy-start(f32[32,128]{1,0:T(8,128)} %get-tuple-element.5.tap_in) | copy-start | bytes 49156
